TPU v7x, 512 devices: a whole 4x8x8 slice. The times are simulated.
512 devices in a mesh: node: 128 (over z, y, core), feat: 4 (over x).
Axes of the slice: x: 4, y: 8, z: 8, core: 2. Of those that a mesh axis runs over, the one named last changes fastest.
Arguments:
- embed: bfloat16 [256, 131072], P('feat', 'node'), may hold values from -6 to 6
- tile_weight: bfloat16 [128, 135, 128, 128], P('node'), may hold values from -0.125 to 0.125
- tile_rows: int32 [128, 135], P('node'), may hold values from 0 to 7
- tile_cols: int32 [128, 135], P('node'), may hold values from 0 to 135, as said below
- send_rows: int32 [128, 128], P('node'), may hold values from 0 to 7
- src_local: int32 [65536], P('node'), may hold values from 0 to 1023
- dst_owner: int32 [65536, 1], P('node'), may hold values from 0 to 127; in each aligned block of 512 rows (0 to 511, 512 to 1023, ...) at most 8 rows name the same one
- dst_local: int32 [65536], P('node'), may hold values from 0 to 1023
- w_in: bfloat16 [256, 1024], P('feat'), may hold values from -0.375 to 0.375
- b_in: float32 [1024], replicated, may hold values from -4 to 4
- w_out: float32 [1024], replicated, may hold values from -0.1875 to 0.1875
Outputs:
- propagated: bfloat16 [256, 131072], P('feat', 'node')
- scores: float32 [65536], P('node')
Inputs may be any that keep to these rules, and one draw needn't show every extreme that they name: In each part, the entries of tile_cols below 8 are the numbers 0 to 7 once each, and tile_rows equals tile_cols at those tiles; the other 127 entries are 8 + p for every part p other than the part itself, once each. `dst_owner`: among the 512 queries of one part, at most 8 have the same destination part, and exactly 8 do for some destination part.
All inputs are finite; a program needn't handle non-finite values.
Results may differ from a plain program's by a relative error of at most 0.015.
Values may be sent and summed in bfloat16 or wider, within the bound.
A program may use at most 64 MiB of HBM per device.

v0:
```python
import jax
import jax.numpy as jnp
from jax import lax
from jax.sharding import PartitionSpec as P

HOPS = 2
TELEPORT = 0.1


def propagate(current, initial, weights, tile_row, tile_col, targets):
    channels, node_count = current.shape
    block_size = weights.shape[-1]
    block_count = node_count // block_size
    blocked = current.reshape(channels, block_count, block_size)
    outgoing = blocked[:, targets, :]
    incoming = lax.all_to_all(outgoing, "node", split_axis=1, concat_axis=1, tiled=True)
    sources = jnp.concatenate([blocked, incoming], axis=1)
    picked = sources[:, tile_col, :]
    products = jnp.einsum("ctj,tij->cti", picked, weights, preferred_element_type=jnp.float32)
    selector = (tile_row[None, :] == jnp.arange(block_count, dtype=jnp.int32)[:, None]).astype(
        jnp.float32
    )
    summed = jnp.einsum("rt,cti->cri", selector, products, precision=lax.Precision.HIGHEST)
    return ((1.0 - TELEPORT) * summed.reshape(channels, node_count) + TELEPORT * initial).astype(
        jnp.bfloat16
    )


def contract_rows(left_matrix, right_matrix):
    return lax.dot_general(
        left_matrix, right_matrix, (((0,), (0,)), ((), ())), preferred_element_type=jnp.float32
    )


def shards(
    embed,
    tile_weight,
    tile_rows,
    tile_cols,
    send_rows,
    src_local,
    dst_owner,
    dst_local,
    w_in,
    b_in,
    w_out,
):
    weights = tile_weight[0]
    tile_row = tile_rows[0]
    tile_col = tile_cols[0]
    targets = send_rows[0]
    initial = embed.astype(jnp.float32)
    current = embed
    for hop_index in range(HOPS):
        current = propagate(current, initial, weights, tile_row, tile_col, targets)
    part_count = lax.axis_size("node")
    queries = src_local.shape[0]
    capacity = max(2, 2 * queries // part_count)
    owners = dst_owner[:, 0]
    owner_hits = (owners[:, None] == jnp.arange(part_count, dtype=jnp.int32)[None, :]).astype(
        jnp.int32
    )
    slot_rank = jnp.sum(jnp.cumsum(owner_hits, axis=0) * owner_hits, axis=1) - 1
    requests = (
        jnp.zeros((part_count * capacity,), jnp.int32)
        .at[owners * capacity + slot_rank]
        .set(dst_local)
    )
    requests = requests.reshape(part_count, capacity)
    replies = lax.all_to_all(
        current[:, lax.all_to_all(requests, "node", split_axis=0, concat_axis=0, tiled=True)],
        "node",
        split_axis=1,
        concat_axis=1,
        tiled=True,
    )
    target_rows = replies[:, owners, slot_rank]
    source_rows = current[:, src_local]
    hadamard = (source_rows.astype(jnp.float32) * target_rows.astype(jnp.float32)).astype(
        jnp.bfloat16
    )
    partial_value = contract_rows(w_in, hadamard)
    hidden = lax.psum(partial_value.astype(jnp.bfloat16), "feat").astype(jnp.float32)
    active = jnp.maximum(hidden + b_in[:, None], 0.0)
    scores = jnp.dot(w_out, active, precision=lax.Precision.HIGHEST)
    return (current, scores)


def solution(mesh):
    placed = (
        P("feat", "node"),
        P("node", None, None, None),
        P("node", None),
        P("node", None),
        P("node", None),
        P("node"),
        P("node", None),
        P("node"),
        P("feat", None),
        P(),
        P(),
    )
    return jax.shard_map(
        shards,
        mesh=mesh,
        in_specs=placed,
        out_specs=(P("feat", "node"), P("node")),
        check_vma=False,
    )
```

profile of v0, /device:TPU:8, one launch (start us, length us, event | category | flops | bytes accessed | tf_op | source)
XLA Modules:
  0.0 273.8 jit_solution(4774526276266268185)
XLA Ops:
  7.2 1.0 copy_bitcast_fusion
  8.1 0.7 fusion.56
  8.8 2.2 gather_fusion
  11.0 17.5 %all-to-all-start = ((bf16[64,128,128]{2,0,1:T(8,128)(2,1)}), bf16[64,128,128]{2,0,1:T(8,128)(2,1)S(1)}, u32[]{:S(2)}, u32[]{:S(2)}) async-start(bf16[64,128,128]{2,0,1:T(8,128)(2,1)} %bitcast.90), calls=%async_computation | async-start | bytes 4194304 | tf_op jit(solution)/shard_map/all_to_all | solution.py:16
  29.1 0.2 fusion.41
  29.4 2.6 scatter_custom_fusion
  32.0 0.7 all_to_all.19
  32.7 49.8 %all-to-all-done = bf16[64,128,128]{2,0,1:T(8,128)(2,1)S(1)} async-done(((bf16[64,128,128]{2,0,1:T(8,128)(2,1)}), bf16[64,128,128]{2,0,1:T(8,128)(2,1)S(1)}, u32[]{:S(2)}, u32[]{:S(2)}) %all-to-all-start) | async-done | bytes 2097184 | tf_op jit(solution)/shard_map/all_to_all | solution.py:16
  82.5 6.1 %all-to-all-start.2 = ((s32[128,1,8]{2,1,0:T(1,128)}), s32[128,1,8]{2,1,0:T(1,128)S(1)}, u32[]{:S(2)}, u32[]{:S(2)}) async-start(s32[128,1,8]{2,1,0:T(1,128)} %bitcast.25), calls=%async_computation.2 | async-start | bytes 131072 | tf_op jit(solution)/shard_map/all_to_all | solution.py:71
  88.6 1.6 pad_maximum_fusion
  90.2 2.6 gather_fusion.1
  92.8 5.4 %fusion.10 = f32[64,135,128]{2,0,1:T(8,128)S(1)} fusion(bf16[1,135,128,128]{3,2,1,0:T(8,128)(2,1)} %param.12, bf16[135,64,128]{2,1,0:T(8,128)(2,1)S(1)} %gather_fusion.1), kind=kOutput, calls=%fused_computation.20 | convolution fusion | flops 283115520 | bytes 11059200 | tf_op jit(solution)/shard_map/ctj,tij->cti/dot_general | solution.py:19
  98.2 4.0 %fusion.34 = f32[64,8,128]{2,1,0:T(8,128)S(1)} fusion(f32[64,135,128]{2,0,1:T(8,128)S(1)} %fusion.10, s32[135]{0:T(256)S(1)} %bitcast.101), kind=kOutput, calls=%fused_computation.31 | convolution fusion | flops 106234936 | bytes 4686364 | tf_op jit(solution)/shard_map/rt,cti->cri/dot_general | solution.py:23
  102.2 0.2 copy.83
  102.7 2.2 gather_fusion.2
  104.8 13.7 %all-to-all-start.1 = ((bf16[64,128,128]{2,0,1:T(8,128)(2,1)}), bf16[64,128,128]{2,0,1:T(8,128)(2,1)S(1)}, u32[]{:S(2)}, u32[]{:S(2)}) async-start(bf16[64,128,128]{2,0,1:T(8,128)(2,1)} %bitcast.13), calls=%async_computation.1 | async-start | bytes 4194304 | tf_op jit(solution)/shard_map/all_to_all | solution.py:16
  118.7 53.9 %all-to-all-done.1 = bf16[64,128,128]{2,0,1:T(8,128)(2,1)S(1)} async-done(((bf16[64,128,128]{2,0,1:T(8,128)(2,1)}), bf16[64,128,128]{2,0,1:T(8,128)(2,1)S(1)}, u32[]{:S(2)}, u32[]{:S(2)}) %all-to-all-start.1) | async-done | bytes 2097184 | tf_op jit(solution)/shard_map/all_to_all | solution.py:16
  172.6 1.6 pad_maximum_fusion.1
  174.2 2.6 gather_fusion.3
  176.8 5.4 %fusion.15 = f32[64,135,128]{2,0,1:T(8,128)S(1)} fusion(bf16[1,135,128,128]{3,2,1,0:T(8,128)(2,1)} %param.12, bf16[135,64,128]{2,1,0:T(8,128)(2,1)S(1)} %gather_fusion.3), kind=kOutput, calls=%fused_computation.21 | convolution fusion | flops 283115520 | bytes 11059200 | tf_op jit(solution)/shard_map/ctj,tij->cti/dot_general | solution.py:19
  182.2 4.0 %fusion.31 = f32[64,8,128]{2,1,0:T(8,128)S(1)} fusion(f32[64,135,128]{2,0,1:T(8,128)S(1)} %fusion.15, s32[135]{0:T(256)S(1)} %bitcast.102), kind=kOutput, calls=%fused_computation.30 | convolution fusion | flops 106234936 | bytes 4686364 | tf_op jit(solution)/shard_map/rt,cti->cri/dot_general | solution.py:23
  186.5 3.2 %gather_fusion.5 = bf16[1024,64]{1,0:T(8,128)(2,1)S(1)} fusion(bf16[64,1024]{0,1:T(8,128)(2,1)S(1)} %fusion.39, s32[1024]{0:T(1024)S(1)} %broadcast_clamp_fusion), kind=kCustom, calls=%fused_computation.5 | custom fusion | bytes 266240 | tf_op jit(solution)/shard_map/gather | solution.py:71
  189.8 0.9 reshape.217
  190.7 6.2 %all-to-all-start.3 = ((bf16[128,2,256]{2,1,0:T(2,128)(2,1)}), bf16[128,2,256]{2,1,0:T(2,128)(2,1)S(1)}, u32[]{:S(2)}, u32[]{:S(2)}) async-start(bf16[128,2,256]{2,1,0:T(2,128)(2,1)} %reshape.217), calls=%async_computation.3 | async-start | bytes 262144 | tf_op jit(solution)/shard_map/all_to_all | solution.py:70
  196.8 0.3 all-reduce.2.cloned.1.call-start
  197.2 1.3 gather_fusion.4
  198.6 10.2 %all-to-all-done.3 = bf16[128,2,256]{2,1,0:T(2,128)(2,1)S(1)} async-done(((bf16[128,2,256]{2,1,0:T(2,128)(2,1)}), bf16[128,2,256]{2,1,0:T(2,128)(2,1)S(1)}, u32[]{:S(2)}, u32[]{:S(2)}) %all-to-all-start.3) | async-done | bytes 131104 | tf_op jit(solution)/shard_map/all_to_all | solution.py:70
  209.0 3.1 %gather_fusion.6 = bf16[512,64]{1,0:T(8,128)(2,1)S(1)} fusion(bf16[64,128,8]{0,2,1:T(8,128)(2,1)S(1)} %bitcast.91, s32[512]{0:T(512)S(1)} %bitcast.89), kind=kCustom, calls=%fused_computation.6 | custom fusion | bytes 135168 | tf_op jit(solution)/shard_map/gather | solution.py:77
  212.1 1.5 fusion.24
  213.6 0.8 copy.82
  214.4 48.7 %all-reduce.2.cloned.1.call-done = bf16[1024,512]{0,1:T(8,128)(2,1)} async-done(((bf16[1024,512]{0,1:T(8,128)(2,1)}), bf16[1024,512]{0,1:T(8,128)(2,1)}) %all-reduce.2.cloned.1.call-update) | async-done | bytes 1048592 | tf_op jit(solution)/shard_map/psum | solution.py:83
  263.1 3.9 %fusion.20 = f32[1,512]{1,0:T(1,128)} fusion(f32[1024,1]{0,1:T(1,128)S(1)} %bitcast.105, bf16[1024,512]{0,1:T(8,128)(2,1)} %all-reduce.2.cloned.1.call-done, f32[1024]{0:T(1024)S(1)} %copy-done.7), kind=kOutput, calls=%fused_computation.22 | convolution fusion | flops 7864320 | bytes 1058816 | tf_op jit(solution)/shard_map/dot_general | solution.py:85
  (43 shorter events, 1.5 us)
Async XLA Ops:
  7.2 204.9 %copy-start = (bf16[64,1024]{1,0:T(8,128)(2,1)S(1)}, bf16[64,1024]{1,0:T(8,128)(2,1)}, u32[]{:S(2)}) copy-start(bf16[64,1024]{1,0:T(8,128)(2,1)} %param.19) | copy-start | bytes 393220
  11.0 17.5 %copy-start.1 = (bf16[64,1024]{1,0:T(8,128)(2,1)S(1)}, bf16[64,1024]{1,0:T(8,128)(2,1)}, u32[]{:S(2)}) copy-start(bf16[64,1024]{1,0:T(8,128)(2,1)} %param.11) | copy-start | bytes 393220
  11.0 17.7 %copy-start.2 = (s32[512,1]{0,1:T(1,128)S(1)}, s32[512,1]{0,1:T(1,128)}, u32[]{:S(2)}) copy-start(s32[512,1]{0,1:T(1,128)} %param.17) | copy-start | bytes 6148
  11.0 21.7 %copy-start.5 = (s32[1,135]{1,0:T(1,128)S(1)}, s32[1,135]{1,0:T(1,128)}, u32[]{:S(2)}) copy-start(s32[1,135]{1,0:T(1,128)} %param.14) | copy-start | bytes 1624
  11.0 71.6 %all-to-all-start = ((bf16[64,128,128]{2,0,1:T(8,128)(2,1)}), bf16[64,128,128]{2,0,1:T(8,128)(2,1)S(1)}, u32[]{:S(2)}, u32[]{:S(2)}) async-start(bf16[64,128,128]{2,0,1:T(8,128)(2,1)} %bitcast.90), calls=%async_computation | async-start | bytes 4194304 | tf_op jit(solution)/shard_map/all_to_all | solution.py:16
  82.5 22.3 %all-to-all-start.2 = ((s32[128,1,8]{2,1,0:T(1,128)}), s32[128,1,8]{2,1,0:T(1,128)S(1)}, u32[]{:S(2)}, u32[]{:S(2)}) async-start(s32[128,1,8]{2,1,0:T(1,128)} %bitcast.25), calls=%async_computation.2 | async-start | bytes 131072 | tf_op jit(solution)/shard_map/all_to_all | solution.py:71
  92.8 5.4 %copy-start.3 = (s32[1,135]{1,0:T(1,128)S(1)}, s32[1,135]{1,0:T(1,128)}, u32[]{:S(2)}) copy-start(s32[1,135]{1,0:T(1,128)} %param.13) | copy-start | bytes 1624
  104.8 67.8 %all-to-all-start.1 = ((bf16[64,128,128]{2,0,1:T(8,128)(2,1)}), bf16[64,128,128]{2,0,1:T(8,128)(2,1)S(1)}, u32[]{:S(2)}, u32[]{:S(2)}) async-start(bf16[64,128,128]{2,0,1:T(8,128)(2,1)} %bitcast.13), calls=%async_computation.1 | async-start | bytes 4194304 | tf_op jit(solution)/shard_map/all_to_all | solution.py:16
  186.5 10.6 %copy-start.4 = (s32[512]{0:T(512)S(1)}, s32[512]{0:T(512)}, u32[]{:S(2)}) copy-start(s32[512]{0:T(512)} %param.16) | copy-start | bytes 6148
  190.7 18.1 %all-to-all-start.3 = ((bf16[128,2,256]{2,1,0:T(2,128)(2,1)}), bf16[128,2,256]{2,1,0:T(2,128)(2,1)S(1)}, u32[]{:S(2)}, u32[]{:S(2)}) async-start(bf16[128,2,256]{2,1,0:T(2,128)(2,1)} %reshape.217), calls=%async_computation.3 | async-start | bytes 262144 | tf_op jit(solution)/shard_map/all_to_all | solution.py:70
  196.8 66.2 %all-reduce.2.cloned.1.call-start = ((), (), s32[]{:S(2)}) async-start(), calls=%async_computation.4 | async-start | bytes 2097152 | tf_op jit(solution)/shard_map/psum | solution.py:83
  198.5 64.6 %copy-start.6 = (f32[1024]{0:T(1024)S(1)}, f32[1024]{0:T(1024)}, u32[]{:S(2)}) copy-start(f32[1024]{0:T(1024)} %param.21) | copy-start | bytes 12292
  198.5 64.5 %copy-start.7 = (f32[1024]{0:T(1024)S(1)}, f32[1024]{0:T(1024)}, u32[]{:S(2)}) copy-start(f32[1024]{0:T(1024)} %param.20) | copy-start | bytes 12292
Sparse Core Ops, SparseCore 0:
  213.7 49.3 all-reduce.1
where the time goes:
time: 274 us
  waiting for transfers between devices  163 us (59%)
  starting transfers between devices  43.8 us (16%)
  local copies, waits for them, and re-layouts  24.4 us (9%)
  matrix products  24.1 us (9%)
  between operations  14.3 us (5%)
  other arithmetic  4.5 us (2%)
    all_to_all x2, waiting for transfers between devices, propagate(): lax.all_to_all(outgoing, 'node', split_axis=1, concat_axis=1, tiled=True)  104 us
    psum x1, waiting for transfers between devices, shards(): lax.psum(partial_value.astype(jnp.bfloat16), 'feat').astype(jnp.float32)  48.7 us
    all_to_all x2, starting transfers between devices, propagate(): lax.all_to_all(outgoing, 'node', split_axis=1, concat_axis=1, tiled=True)  31.2 us
    dot_general x2, matrix products, propagate(): jnp.einsum('ctj,tij->cti', picked, weights, preferred_element_type=jnp.fl...  10.8 us
    all_to_all x1, waiting for transfers between devices, shards(): lax.all_to_all(current[:, lax.all_to_all(requests, 'node', split_axis=0,...  10.2 us
    dot_general x2, matrix products, propagate(): jnp.einsum('rt,cti->cri', selector, products, precision=lax.Precision.HIG...  7.96 us
    all_to_all x1, starting transfers between devices, shards(): lax.all_to_all(current[:, lax.all_to_all(requests, 'node', split_axis=0,...  6.16 us
    all_to_all x1, starting transfers between devices, shards(): lax.all_to_all(requests, 'node', split_axis=0, concat_axis=0, tiled=True)  6.07 us
  transfers between devices with their start and end apart: 5, of which 4 were waited for; matrix products, arithmetic and copies ran while one was open for 8% of the time, Pallas kernels for 0%

commit v1 on v0

--- a/solution.py
+++ b/solution.py
@@ -45,6 +45,11 @@
     b_in,
     w_out,
 ):
+
+    def turns_match(z_in, ax_name):
+        far_arr = lax.all_gather(z_in, axis_name=ax_name).sum(axis=0)
+        return far_arr
+
     weights = tile_weight[0]
     tile_row = tile_rows[0]
     tile_col = tile_cols[0]
@@ -80,7 +85,7 @@
         jnp.bfloat16
     )
     partial_value = contract_rows(w_in, hadamard)
-    hidden = lax.psum(partial_value.astype(jnp.bfloat16), "feat").astype(jnp.float32)
+    hidden = turns_match(partial_value.astype(jnp.bfloat16), "feat").astype(jnp.float32)
     active = jnp.maximum(hidden + b_in[:, None], 0.0)
     scores = jnp.dot(w_out, active, precision=lax.Precision.HIGHEST)
     return (current, scores)

time: 274 us -> 286 us (1.044)
  the two profiles are of different devices: /device:TPU:8 before, /device:TPU:1 now
where the time goes in v1:
time: 286 us
  waiting for transfers between devices  154 us (54%)
  starting transfers between devices  50.4 us (18%)
  local copies, waits for them, and re-layouts  32.2 us (11%)
  matrix products  22.8 us (8%)
  between operations  14.3 us (5%)
  other arithmetic  11.8 us (4%)
    all_to_all x2, waiting for transfers between devices, propagate(): lax.all_to_all(outgoing, 'node', split_axis=1, concat_axis=1, tiled=True)  98.2 us
    all_gather x1, waiting for transfers between devices, turns_match(): far_arr = lax.all_gather(z_in, axis_name=ax_name).sum(axis=0)  44.9 us
    all_to_all x2, starting transfers between devices, propagate(): lax.all_to_all(outgoing, 'node', split_axis=1, concat_axis=1, tiled=True)  32.3 us
    all_to_all x1, waiting for transfers between devices, shards(): lax.all_to_all(current[:, lax.all_to_all(requests, 'node', split_axis=0,...  11 us
    dot_general x2, matrix products, propagate(): jnp.einsum('ctj,tij->cti', picked, weights, preferred_element_type=jnp.fl...  10.8 us
    all_to_all x1, starting transfers between devices, shards(): lax.all_to_all(current[:, lax.all_to_all(requests, 'node', split_axis=0,...  8.95 us
    all_to_all x1, starting transfers between devices, shards(): lax.all_to_all(requests, 'node', split_axis=0, concat_axis=0, tiled=True)  8.85 us
    dot_general x2, matrix products, propagate(): jnp.einsum('rt,cti->cri', selector, products, precision=lax.Precision.HIG...  7.96 us
  transfers between devices with their start and end apart: 5, of which 4 were waited for; matrix products, arithmetic and copies ran while one was open for 8% of the time, Pallas kernels for 0%

profile of v1, /device:TPU:1, one launch (start us, length us, event | category | flops | bytes accessed | tf_op | source)
XLA Modules:
  0.0 285.6 jit_solution(9460009023067622506)
XLA Ops:
  7.2 0.7 fusion.56
  7.9 0.9 copy_bitcast_fusion
  8.8 2.2 gather_fusion
  11.0 18.6 %all-to-all-start = ((bf16[64,128,128]{2,0,1:T(8,128)(2,1)}), bf16[64,128,128]{2,0,1:T(8,128)(2,1)S(1)}, u32[]{:S(2)}, u32[]{:S(2)}) async-start(bf16[64,128,128]{2,0,1:T(8,128)(2,1)} %bitcast.93), calls=%async_computation | async-start | bytes 4194304 | tf_op jit(solution)/shard_map/all_to_all | solution.py:16
  30.4 2.6 scatter_custom_fusion
  33.0 0.7 all_to_all.19
  33.8 47.0 %all-to-all-done = bf16[64,128,128]{2,0,1:T(8,128)(2,1)S(1)} async-done(((bf16[64,128,128]{2,0,1:T(8,128)(2,1)}), bf16[64,128,128]{2,0,1:T(8,128)(2,1)S(1)}, u32[]{:S(2)}, u32[]{:S(2)}) %all-to-all-start) | async-done | bytes 2097184 | tf_op jit(solution)/shard_map/all_to_all | solution.py:16
  80.8 8.9 %all-to-all-start.2 = ((s32[128,1,8]{2,1,0:T(1,128)}), s32[128,1,8]{2,1,0:T(1,128)S(1)}, u32[]{:S(2)}, u32[]{:S(2)}) async-start(s32[128,1,8]{2,1,0:T(1,128)} %bitcast.25), calls=%async_computation.2 | async-start | bytes 131072 | tf_op jit(solution)/shard_map/all_to_all | solution.py:76
  89.7 1.6 pad_maximum_fusion
  91.2 2.6 gather_fusion.1
  93.9 5.4 %fusion.10 = f32[64,135,128]{2,0,1:T(8,128)S(1)} fusion(bf16[1,135,128,128]{3,2,1,0:T(8,128)(2,1)} %param.12, bf16[135,64,128]{2,1,0:T(8,128)(2,1)S(1)} %gather_fusion.1), kind=kOutput, calls=%fused_computation.20 | convolution fusion | flops 283115520 | bytes 11059200 | tf_op jit(solution)/shard_map/ctj,tij->cti/dot_general | solution.py:19
  99.3 4.0 %fusion.34 = f32[64,8,128]{2,1,0:T(8,128)S(1)} fusion(f32[64,135,128]{2,0,1:T(8,128)S(1)} %fusion.10, s32[135]{0:T(256)S(1)} %bitcast.104), kind=kOutput, calls=%fused_computation.31 | convolution fusion | flops 106234936 | bytes 4686364 | tf_op jit(solution)/shard_map/rt,cti->cri/dot_general | solution.py:23
  103.7 2.2 gather_fusion.2
  105.9 13.7 %all-to-all-start.1 = ((bf16[64,128,128]{2,0,1:T(8,128)(2,1)}), bf16[64,128,128]{2,0,1:T(8,128)(2,1)S(1)}, u32[]{:S(2)}, u32[]{:S(2)}) async-start(bf16[64,128,128]{2,0,1:T(8,128)(2,1)} %bitcast.13), calls=%async_computation.1 | async-start | bytes 4194304 | tf_op jit(solution)/shard_map/all_to_all | solution.py:16
  119.8 51.1 %all-to-all-done.1 = bf16[64,128,128]{2,0,1:T(8,128)(2,1)S(1)} async-done(((bf16[64,128,128]{2,0,1:T(8,128)(2,1)}), bf16[64,128,128]{2,0,1:T(8,128)(2,1)S(1)}, u32[]{:S(2)}, u32[]{:S(2)}) %all-to-all-start.1) | async-done | bytes 2097184 | tf_op jit(solution)/shard_map/all_to_all | solution.py:16
  170.9 1.6 pad_maximum_fusion.1
  172.5 2.6 gather_fusion.3
  175.1 5.4 %fusion.15 = f32[64,135,128]{2,0,1:T(8,128)S(1)} fusion(bf16[1,135,128,128]{3,2,1,0:T(8,128)(2,1)} %param.12, bf16[135,64,128]{2,1,0:T(8,128)(2,1)S(1)} %gather_fusion.3), kind=kOutput, calls=%fused_computation.21 | convolution fusion | flops 283115520 | bytes 11059200 | tf_op jit(solution)/shard_map/ctj,tij->cti/dot_general | solution.py:19
  180.5 4.0 %fusion.31 = f32[64,8,128]{2,1,0:T(8,128)S(1)} fusion(f32[64,135,128]{2,0,1:T(8,128)S(1)} %fusion.15, s32[135]{0:T(256)S(1)} %bitcast.105), kind=kOutput, calls=%fused_computation.30 | convolution fusion | flops 106234936 | bytes 4686364 | tf_op jit(solution)/shard_map/rt,cti->cri/dot_general | solution.py:23
  184.8 3.2 %gather_fusion.5 = bf16[1024,64]{1,0:T(8,128)(2,1)S(1)} fusion(bf16[64,1024]{0,1:T(8,128)(2,1)S(1)} %fusion.39, s32[1024]{0:T(1024)S(1)} %broadcast_clamp_fusion), kind=kCustom, calls=%fused_computation.5 | custom fusion | bytes 266240 | tf_op jit(solution)/shard_map/gather | solution.py:76
  188.1 0.9 reshape.218
  188.9 8.9 %all-to-all-start.3 = ((bf16[128,2,256]{2,1,0:T(2,128)(2,1)}), bf16[128,2,256]{2,1,0:T(2,128)(2,1)S(1)}, u32[]{:S(2)}, u32[]{:S(2)}) async-start(bf16[128,2,256]{2,1,0:T(2,128)(2,1)} %reshape.218), calls=%async_computation.3 | async-start | bytes 262144 | tf_op jit(solution)/shard_map/all_to_all | solution.py:75
  197.9 0.3 all-gather.3.cloned.1.call-start
  198.2 1.3 gather_fusion.4
  199.6 11.0 %all-to-all-done.3 = bf16[128,2,256]{2,1,0:T(2,128)(2,1)S(1)} async-done(((bf16[128,2,256]{2,1,0:T(2,128)(2,1)}), bf16[128,2,256]{2,1,0:T(2,128)(2,1)S(1)}, u32[]{:S(2)}, u32[]{:S(2)}) %all-to-all-start.3) | async-done | bytes 131104 | tf_op jit(solution)/shard_map/all_to_all | solution.py:75
  210.8 3.1 %gather_fusion.6 = bf16[512,64]{1,0:T(8,128)(2,1)S(1)} fusion(bf16[64,128,8]{0,2,1:T(8,128)(2,1)S(1)} %bitcast.94, s32[512]{0:T(512)S(1)} %bitcast.92), kind=kCustom, calls=%fused_computation.6 | custom fusion | bytes 135168 | tf_op jit(solution)/shard_map/gather | solution.py:82
  213.9 1.4 fusion.24
  215.3 0.8 copy.82
  216.1 44.9 %all-gather.3.cloned.1.call-done = bf16[4096,512]{0,1:T(8,128)(2,1)} async-done(((bf16[1024,512]{0,1:T(8,128)(2,1)}), bf16[4096,512]{0,1:T(8,128)(2,1)}) %all-gather.3.cloned.1.call-update) | async-done | bytes 4194320 | tf_op jit(solution)/shard_map/all_gather | solution.py:50
  261.0 7.9 %reshape.210 = bf16[4,1024,512]{1,0,2:T(4,128)(2,1)} reshape(bf16[4096,512]{0,1:T(8,128)(2,1)} %all-gather.3.cloned.1.call-done) | data formatting | bytes 8388608 | tf_op jit(solution)/shard_map/all_gather | solution.py:50
  268.8 7.3 %reduce_sum.22 = bf16[1024,512]{0,1:T(8,128)(2,1)S(1)} reduce(bf16[4,1024,512]{1,0,2:T(4,128)(2,1)} %reshape.210, bf16[]{:T(256)} %constant.8.clone.1), dimensions={0}, to_apply=%region_4.5 | reduce | flops 1572864 | bytes 5242882 | tf_op jit(solution)/shard_map/reduce_sum | solution.py:50
  276.1 2.6 fusion.20
  (45 shorter events, 2.0 us)
Async XLA Ops:
  7.2 206.7 %copy-start = (bf16[64,1024]{1,0:T(8,128)(2,1)S(1)}, bf16[64,1024]{1,0:T(8,128)(2,1)}, u32[]{:S(2)}) copy-start(bf16[64,1024]{1,0:T(8,128)(2,1)} %param.19) | copy-start | bytes 393220
  11.0 18.6 %copy-start.1 = (bf16[64,1024]{1,0:T(8,128)(2,1)S(1)}, bf16[64,1024]{1,0:T(8,128)(2,1)}, u32[]{:S(2)}) copy-start(bf16[64,1024]{1,0:T(8,128)(2,1)} %param.11) | copy-start | bytes 393220
  11.0 18.7 %copy-start.2 = (s32[512,1]{0,1:T(1,128)S(1)}, s32[512,1]{0,1:T(1,128)}, u32[]{:S(2)}) copy-start(s32[512,1]{0,1:T(1,128)} %param.17) | copy-start | bytes 6148
  11.0 22.8 %copy-start.5 = (s32[1,135]{1,0:T(1,128)S(1)}, s32[1,135]{1,0:T(1,128)}, u32[]{:S(2)}) copy-start(s32[1,135]{1,0:T(1,128)} %param.14) | copy-start | bytes 1624
  11.0 69.8 %all-to-all-start = ((bf16[64,128,128]{2,0,1:T(8,128)(2,1)}), bf16[64,128,128]{2,0,1:T(8,128)(2,1)S(1)}, u32[]{:S(2)}, u32[]{:S(2)}) async-start(bf16[64,128,128]{2,0,1:T(8,128)(2,1)} %bitcast.93), calls=%async_computation | async-start | bytes 4194304 | tf_op jit(solution)/shard_map/all_to_all | solution.py:16
  80.8 25.1 %all-to-all-start.2 = ((s32[128,1,8]{2,1,0:T(1,128)}), s32[128,1,8]{2,1,0:T(1,128)S(1)}, u32[]{:S(2)}, u32[]{:S(2)}) async-start(s32[128,1,8]{2,1,0:T(1,128)} %bitcast.25), calls=%async_computation.2 | async-start | bytes 131072 | tf_op jit(solution)/shard_map/all_to_all | solution.py:76
  93.9 5.4 %copy-start.3 = (s32[1,135]{1,0:T(1,128)S(1)}, s32[1,135]{1,0:T(1,128)}, u32[]{:S(2)}) copy-start(s32[1,135]{1,0:T(1,128)} %param.13) | copy-start | bytes 1624
  105.9 65.0 %all-to-all-start.1 = ((bf16[64,128,128]{2,0,1:T(8,128)(2,1)}), bf16[64,128,128]{2,0,1:T(8,128)(2,1)S(1)}, u32[]{:S(2)}, u32[]{:S(2)}) async-start(bf16[64,128,128]{2,0,1:T(8,128)(2,1)} %bitcast.13), calls=%async_computation.1 | async-start | bytes 4194304 | tf_op jit(solution)/shard_map/all_to_all | solution.py:16
  184.8 13.4 %copy-start.4 = (s32[512]{0:T(512)S(1)}, s32[512]{0:T(512)}, u32[]{:S(2)}) copy-start(s32[512]{0:T(512)} %param.16) | copy-start | bytes 6148
  188.9 21.7 %all-to-all-start.3 = ((bf16[128,2,256]{2,1,0:T(2,128)(2,1)}), bf16[128,2,256]{2,1,0:T(2,128)(2,1)S(1)}, u32[]{:S(2)}, u32[]{:S(2)}) async-start(bf16[128,2,256]{2,1,0:T(2,128)(2,1)} %reshape.218), calls=%async_computation.3 | async-start | bytes 262144 | tf_op jit(solution)/shard_map/all_to_all | solution.py:75
  197.9 63.1 %all-gather.3.cloned.1.call-start = ((), (), s32[]{:S(2)}) async-start(), calls=%async_computation.4 | async-start | bytes 5242880 | tf_op jit(solution)/shard_map/all_gather | solution.py:50
  268.8 7.3 %copy-start.6 = (f32[1024]{0:T(1024)S(1)}, f32[1024]{0:T(1024)}, u32[]{:S(2)}) copy-start(f32[1024]{0:T(1024)} %param.21) | copy-start | bytes 12292
  268.8 7.3 %copy-start.7 = (f32[1024]{0:T(1024)S(1)}, f32[1024]{0:T(1024)}, u32[]{:S(2)}) copy-start(f32[1024]{0:T(1024)} %param.20) | copy-start | bytes 12292
Sparse Core Ops, SparseCore 0:
  215.4 45.4 all-gather.2
